TPU v7x, 32 devices: a whole 2x2x4 slice. The times are simulated.
32 devices in a mesh: dp: 8 (over z, x), seq: 4 (over y, core).
Axes of the slice: x: 2, y: 2, z: 4, core: 2. Of those that a mesh axis runs over, the one named last changes fastest.
Arguments:
- tiles: bfloat16 [8, 1536, 1536], P('dp', 'seq'), may hold values from -24 to 24
- tile_counts: int32 [8, 4], P('dp'), may hold values from 96 to 384, as said below
- norm_gain: float32 [1536], replicated, may hold values from 0.5 to 8
- qkv_weight: bfloat16 [1536, 2304], P('dp'), may hold values from -1 to 1
Outputs:
- context: bfloat16 [8, 1536, 768], P('dp', 'seq')
Inputs may be any that keep to these rules, and one draw needn't show every extreme that they name: `tile_counts`: every slide has one block with exactly 384 tissue tiles.
All inputs are finite; a program needn't handle non-finite values.
Results may differ from a plain program's by a relative error of at most 0.017.
The roundings to bfloat16 on the way count: a program that leaves them out, or rounds other values in their place, can miss the bound.
Values may be sent and summed in bfloat16 or wider, within the bound.
No kernel may reach another device: no remote copies, remote signals or barrier semaphores. Data moves between devices by JAX's collectives and lax.ppermute only.
A program may use at most 64 MiB of HBM per device.

v0:
```python
import jax
import jax.numpy as jnp
from jax import lax
from jax.sharding import PartitionSpec as P

HEADS = 6
MID_RATE = 4
NEG = -1e30
EPS = 1e-05


def from_partner(value, axis, bit):
    mask = 2**bit
    pairs = [(source, source ^ mask) for source in range(lax.axis_size(axis))]
    return lax.ppermute(value, axis, pairs)


def layer_norm(rows_in, gain):
    floats = rows_in.astype(jnp.float32)
    center = floats - jnp.mean(floats, axis=-1, keepdims=True)
    spread_sq = jnp.mean(center * center, axis=-1, keepdims=True)
    return (center * lax.rsqrt(spread_sq + EPS) * gain).astype(jnp.bfloat16)


def sample_rows(array, stride):
    shaped = array.reshape((array.shape[0] // stride, stride) + array.shape[1:])
    return jnp.stack([shaped[:, head_idx % stride, head_idx] for head_idx in range(array.shape[1])])


def attend(queries, keys, values_in, key_live, scale):
    scores = (
        jnp.einsum("hsqd,hskd->hsqk", queries, keys, preferred_element_type=jnp.float32) * scale
    )
    scores = jnp.where(key_live[:, :, None, :], scores, NEG)
    top = jnp.max(scores, axis=-1)
    expo = jnp.exp(scores - top[..., None])
    denom = jnp.sum(expo, axis=-1)
    weights = (expo / denom[..., None]).astype(jnp.bfloat16)
    result = jnp.einsum("hsqk,hskd->hsqd", weights, values_in, preferred_element_type=jnp.float32)
    return (result, top + jnp.log(denom))


def spread(result, log_total, stride):
    heads_n = result.shape[0]
    count_n = result.shape[1]
    onehot = (
        jnp.arange(stride, dtype=jnp.int32)[None, :]
        == (jnp.arange(heads_n, dtype=jnp.int32) % stride)[:, None]
    )
    full_ctx = (result[:, :, None, :] * onehot[:, None, :, None].astype(result.dtype)).reshape(
        heads_n, count_n * stride, result.shape[2]
    )
    chosen = jnp.broadcast_to(onehot[:, None, :], (heads_n, count_n, stride)).reshape(
        heads_n, count_n * stride
    )
    full_lt = jnp.where(chosen, jnp.repeat(log_total, stride, axis=1), NEG)
    return (full_ctx, full_lt)


def combine(contexts, totals):
    stacked_lt = jnp.stack(totals)
    top = jnp.max(stacked_lt, axis=0)
    wts = jnp.exp(stacked_lt - top)
    stacked_ctx = jnp.stack(contexts)
    return jnp.sum(wts[..., None] * stacked_ctx, axis=0) / jnp.sum(wts, axis=0)[..., None]


def key_alive(owners, within, counts, stride, heads_n):
    seq_n = counts.shape[0]
    owner_count = jnp.sum(
        jnp.where(
            owners[:, None] == jnp.arange(seq_n, dtype=jnp.int32)[None, :], counts[None, :], 0
        ),
        axis=1,
    )
    offsets = jnp.arange(heads_n, dtype=jnp.int32) % stride
    slots = offsets[:, None] + stride * within[None, :]
    return slots < owner_count[None, :]


def sampled_attention(queries, gathered, alive, stride, scale):
    heads_n = queries.shape[0]
    per_dev = queries.shape[1]
    result, log_total = attend(
        queries[:, None], gathered[0][:, None], gathered[1][:, None], alive[:, None], scale
    )
    return spread(
        result.reshape(heads_n, per_dev, result.shape[3]),
        log_total.reshape(heads_n, per_dev),
        stride,
    )


def local(tiles, tile_counts, norm_gain, qkv_weight):
    rows_in = tiles[0]
    counts = tile_counts[0]
    tok_dev = rows_in.shape[0]
    seq_n = lax.axis_size("seq")
    my_index = lax.axis_index("seq")
    dev_ids = jnp.arange(seq_n, dtype=jnp.int32)
    my_count = jnp.sum(jnp.where(dev_ids == my_index, counts, 0))
    is_live = jnp.arange(tok_dev, dtype=jnp.int32) < my_count
    normed = layer_norm(rows_in, norm_gain)
    width3 = qkv_weight.shape[1]
    width = width3 // 3
    heads_n = HEADS
    head_dim = width // heads_n
    scale = head_dim ** (-0.5)
    qkv = jnp.dot(
        normed,
        lax.all_gather(qkv_weight, "dp", axis=0, tiled=True),
        preferred_element_type=jnp.float32,
    ).astype(jnp.bfloat16)
    queries = qkv[:, :width].reshape(tok_dev, heads_n, head_dim)
    keys = qkv[:, width : 2 * width].reshape(tok_dev, heads_n, head_dim)
    values_in = qkv[:, 2 * width :].reshape(tok_dev, heads_n, head_dim)
    local_live = jnp.broadcast_to(is_live[None, None, :], (heads_n, 1, tok_dev))
    local_ctx, local_lt = attend(
        queries.transpose(1, 0, 2)[:, None],
        keys.transpose(1, 0, 2)[:, None],
        values_in.transpose(1, 0, 2)[:, None],
        local_live,
        scale,
    )
    local_ctx = local_ctx.reshape(heads_n, tok_dev, head_dim)
    local_lt = local_lt.reshape(heads_n, tok_dev)
    mid_stride = MID_RATE
    mid_rows = tok_dev // mid_stride
    q_mid = sample_rows(queries, mid_stride)
    kv_mid = jnp.stack([sample_rows(keys, mid_stride), sample_rows(values_in, mid_stride)])
    bit_count = MID_RATE.bit_length() - 1
    bit_order = list(range(bit_count))
    mid_keys = kv_mid
    source_ids = jnp.reshape(my_index, (1,))
    for bit_pos in bit_order:
        partner_keys = from_partner(mid_keys, "seq", bit_pos)
        mid_keys = jnp.concatenate([mid_keys, partner_keys], axis=2)
        source_ids = jnp.concatenate([source_ids, source_ids ^ 1 << bit_pos])
    mid_owners = jnp.repeat(source_ids, mid_rows, total_repeat_length=mid_stride * mid_rows)
    mid_within = jnp.tile(jnp.arange(mid_rows, dtype=jnp.int32), mid_stride)
    mid_alive = key_alive(mid_owners, mid_within, counts, mid_stride, heads_n)
    mid_ctx, mid_lt = sampled_attention(q_mid, mid_keys, mid_alive, mid_stride, scale)
    wide_rows = tok_dev // seq_n
    q_wide = sample_rows(queries, seq_n)
    kv_wide = jnp.stack([sample_rows(keys, seq_n), sample_rows(values_in, seq_n)])
    wide_keys = lax.all_gather(kv_wide, "seq", axis=2, tiled=True)
    wide_owners = jnp.arange(seq_n * wide_rows, dtype=jnp.int32) // wide_rows
    wide_within = jnp.arange(seq_n * wide_rows, dtype=jnp.int32) % wide_rows
    wide_alive = key_alive(wide_owners, wide_within, counts, seq_n, heads_n)
    wide_ctx, wide_lt = sampled_attention(q_wide, wide_keys, wide_alive, seq_n, scale)
    mixed = combine([local_ctx, mid_ctx, wide_ctx], [local_lt, mid_lt, wide_lt])
    mixed = jnp.where(is_live[None, :, None], mixed, 0.0)
    return mixed.transpose(1, 0, 2).reshape(tok_dev, width).astype(jnp.bfloat16)[None]


def solution(mesh):
    return jax.shard_map(
        local,
        mesh=mesh,
        in_specs=(P("dp", "seq", None), P("dp", None), P(), P("dp", None)),
        out_specs=P("dp", "seq", None),
        check_vma=False,
    )
```

profile of v0, /device:TPU:0, one launch (start us, length us, event | category | flops | bytes accessed | tf_op | source)
XLA Modules:
  0.0 174.4 jit_solution(12791462369132801549)
XLA Ops:
  6.5 0.0 all-gather.3.cloned.1.call-start
  6.5 0.7 all-gather.3.cloned.1.call-update
  7.3 0.0 all-gather.5.cloned.1.call-start
  7.3 0.1 mul.121
  7.4 0.6 iota_compare_fusion.2
  8.1 0.2 mul.129
  8.2 0.1 add_xor_fusion
  8.3 1.4 fusion.37
  9.7 1.2 iota_compare_fusion.3
  10.9 0.7 fusion.47
  11.6 2.1 %add_select_fusion = (s32[384]{0:T(512)S(1)}, s32[384]{0:T(512)S(1)}) fusion(pred[384]{0:T(512)(128)(4,1)} %constant.173, pred[384]{0:T(512)(128)(4,1)} %constant.174, pred[384]{0:T(512)(128)(4,1)} %constant.175, s32[]{:T(128)} %axis_index.12, s32[]{:T(128)} %bitcast.10, s32[]{:T(128)} %bitcast.9, s32[]{:T(128)} %bitcast.8), kind=kLoop, calls=%fused_computation.103 | loop fusion | flops 4224 | bytes 4240 | tf_op jit(solution)/shard_map/jit(floor_divide)/jit(_where)/select_n | solution.py:147
  13.6 0.7 select_reduce_fusion.1
  14.4 0.2 convert_reduce_fusion
  14.6 0.5 fusion.6
  15.1 0.7 add_compare_fusion.1
  15.8 104.8 %all-gather.3.cloned.1.call-done = bf16[1536,2304]{1,0:T(8,128)(2,1)} async-done(((bf16[192,2304]{1,0:T(8,128)(2,1)}), bf16[1536,2304]{1,0:T(8,128)(2,1)}) %all-gather.3.cloned.1.call-update) | async-done | bytes 7077904 | tf_op jit(solution)/shard_map/all_gather | solution.py:111
  120.6 0.0 copy-done.8
  120.6 6.1 %convolution_convert_fusion = bf16[384,2304]{1,0:T(8,128)(2,1)S(1)} fusion(bf16[1536,2304]{1,0:T(8,128)(2,1)} %all-gather.3.cloned.1.call-done, bf16[1,384,1536]{2,1,0:T(8,128)(2,1)S(1)} %copy-done, f32[1536]{0:T(1024)S(1)} %copy-done.8, f32[384]{0:T(512)S(1)} %add_rsqrt_fusion, f32[384]{0:T(512)S(1)} %broadcast_multiply_fusion.2), kind=kOutput, calls=%fused_computation | convolution fusion | flops 2721742848 | bytes 10036224 | tf_op jit(solution)/shard_map/dot_general | solution.py:109
  126.6 0.1 fusion.43
  126.8 0.7 reshape_reshape.14
  127.4 0.3 fusion.46
  127.7 0.7 reshape_reshape.13
  128.4 0.3 fusion.45
  128.9 0.7 pad_maximum_fusion.2
  129.6 0.0 collective-permute-start
  129.6 0.0 all-gather.5.cloned.1.call-update
  129.6 0.3 copy.82
  129.9 0.7 reshape_reshape.12
  130.6 0.3 copy.80
  130.9 0.3 copy.102
  131.2 0.9 fusion.44
  132.2 0.3 copy.83
  132.5 0.3 copy.81
  132.8 1.1 copy.103
  134.0 0.0 copy-done.6
  134.0 0.7 fusion.1
  134.7 0.0 copy-start.1
  134.7 0.8 fusion.2
  135.5 0.0 collective-permute-done
  135.5 1.0 pad_maximum_fusion.1
  136.5 1.6 collective-permute-start.1
  138.2 0.0 copy-done.1
  138.2 1.3 fusion.10
  139.5 17.2 %collective-permute-done.1 = bf16[2,6,192,128]{3,2,1,0:T(8,128)(2,1)S(1)} collective-permute-done((bf16[2,6,192,128]{3,2,1,0:T(8,128)(2,1)S(1)}, bf16[2,6,192,128]{3,2,1,0:T(8,128)(2,1)S(1)}, u32[]{:S(2)}, u32[]{:S(2)}) %collective-permute-start.1) | collective-permute-done | bytes 589856 | tf_op jit(solution)/shard_map/ppermute | solution.py:15
  156.7 1.0 pad_maximum_fusion
  157.8 0.5 fusion.48
  158.3 0.4 fusion.19
  158.6 0.5 fusion.22
  159.2 0.0 all-gather.5.cloned.1.call-done
  159.2 1.5 fusion.49
  160.8 0.4 fusion.20
  161.2 0.2 broadcast_select_fusion.1
  161.4 0.2 select_n.153
  161.6 0.2 select_n.151
  161.8 0.2 select_n.152
  161.9 0.2 select_n.145
  162.2 1.4 fusion.21
  163.6 0.2 mul.126
  163.8 0.2 mul.132
  164.0 0.4 broadcast_multiply_fusion.1
  164.5 1.2 fusion
  165.7 0.4 fusion.15
  166.1 0.3 copy.105
  166.5 1.1 copy.106
  (42 shorter events, 0.3 us)
Async XLA Ops:
  6.5 7.9 %copy-start = (bf16[1,384,1536]{2,1,0:T(8,128)(2,1)S(1)}, bf16[1,384,1536]{2,1,0:T(8,128)(2,1)}, u32[]{:S(2)}) copy-start(bf16[1,384,1536]{2,1,0:T(8,128)(2,1)} %param.6) | copy-start | bytes 3538948
  6.5 114.0 %copy-start.8 = (f32[1536]{0:T(1024)S(1)}, f32[1536]{0:T(1024)}, u32[]{:S(2)}) copy-start(f32[1536]{0:T(1024)} %param.8) | copy-start | bytes 18436
  6.5 114.0 %all-gather.3.cloned.1.call-start = ((), (), s32[]{:S(2)}) async-start(), calls=%async_computation | async-start | bytes 7962624 | tf_op jit(solution)/shard_map/all_gather | solution.py:111
  7.3 152.0 %all-gather.5.cloned.1.call-start = ((), (), s32[]{:S(2)}) async-start(), calls=%async_computation.1 | async-start | bytes 1474560 | tf_op jit(solution)/shard_map/all_gather | solution.py:146
  129.6 5.9 %collective-permute-start = (bf16[2,6,96,128]{3,2,1,0:T(8,128)(2,1)}, bf16[2,6,96,128]{3,2,1,0:T(8,128)(2,1)}, u32[]{:S(2)}, u32[]{:S(2)}) collective-permute-start(bf16[2,6,96,128]{3,2,1,0:T(8,128)(2,1)} %pad_maximum_fusion.2), channel_id=1, source_target_pairs={{0,1},{1,0},{2,3},{3,2},{4,5},{5,4},{6,7},{7,6},{8,9},{9,8},{10,11... | collective-permute-start | bytes 884744 | tf_op jit(solution)/shard_map/ppermute | solution.py:15
  132.1 1.7 copy-start.4
  132.1 1.7 copy-start.3
  132.1 1.8 %copy-start.2 = (bf16[96,1,1,128]{3,2,1,0:T(2,128)(2,1)S(1)}, bf16[96,1,1,128]{3,2,1,0:T(2,128)(2,1)}, u32[]{:S(2)}) copy-start(bf16[96,1,1,128]{3,2,1,0:T(2,128)(2,1)} %get-tuple-element.26) | copy-start | bytes 73732
  132.2 1.8 %copy-start.6 = (pred[384]{0:T(512)(128)(4,1)S(1)}, pred[384]{0:T(512)(128)(4,1)}, u32[]{:S(2)}) copy-start(pred[384]{0:T(512)(128)(4,1)} %iota_compare_fusion.3) | copy-start | bytes 1156
  134.7 3.5 %copy-start.1 = (bf16[384,6,128]{2,0,1:T(8,128)(2,1)S(1)}, bf16[384,6,128]{2,0,1:T(8,128)(2,1)}, u32[]{:S(2)}) copy-start(bf16[384,6,128]{2,0,1:T(8,128)(2,1)} %copy.103) | copy-start | bytes 1769476
  136.5 20.2 %collective-permute-start.1 = (bf16[2,6,192,128]{3,2,1,0:T(8,128)(2,1)S(1)}, bf16[2,6,192,128]{3,2,1,0:T(8,128)(2,1)S(1)}, u32[]{:S(2)}, u32[]{:S(2)}) collective-permute-start(bf16[2,6,192,128]{3,2,1,0:T(8,128)(2,1)S(1)} %pad_maximum_fusion.1), channel_id=1, source_target_pairs={{0,2},{1,3},{2,0},{3,1},{4,6},{5,7},{6,4},{7,5},{8,10},{9,11},{10,... | collective-permute-start | bytes 1769480 | tf_op jit(solution)/shard_map/ppermute | solution.py:15
  139.5 18.3 %copy-start.5 = (pred[6,384]{1,0:T(8,128)(4,1)S(1)}, pred[6,384]{1,0:T(8,128)(4,1)}, u32[]{:S(2)}) copy-start(pred[6,384]{1,0:T(8,128)(4,1)} %get-tuple-element.50) | copy-start | bytes 6916
  159.2 2.0 %copy-start.7 = (pred[6,4]{1,0:T(8,128)(4,1)S(1)}, pred[6,4]{1,0:T(8,128)(4,1)}, u32[]{:S(2)}) copy-start(pred[6,4]{1,0:T(8,128)(4,1)} %get-tuple-element.48) | copy-start | bytes 76
Sparse Core Ops, SparseCore 0:
  9.5 110.9 all-gather.2
  129.8 20.2 all-gather.4
where the time goes:
time: 175 us; the launch traced here: 174 us
  waiting for transfers between devices  123 us (70%)
  other arithmetic  14.2 us (8%)
  between operations  13.8 us (8%)
  matrix products  12 us (7%)
  local copies, waits for them, and re-layouts  9.92 us (6%)
    all_gather x1, waiting for transfers between devices, local(): lax.all_gather(qkv_weight, 'dp', axis=0, tiled=True)  105 us
    ppermute x2, waiting for transfers between devices, from_partner(): return lax.ppermute(value, axis, pairs)  17.2 us
    dot_general x1, matrix products, local(): jnp.dot(normed, lax.all_gather(qkv_weight, 'dp', axis=0, tiled=True), pre...  6.07 us
  transfers between devices with their start and end apart: 4, of which 2 were waited for; matrix products, arithmetic and copies ran while one was open for 11% of the time, Pallas kernels for 0%

commit v1 on v0

--- a/solution.py
+++ b/solution.py
@@ -2,6 +2,7 @@
 import jax.numpy as jnp
 from jax import lax
 from jax.sharding import PartitionSpec as P
+from jax.lax import all_to_all, axis_size
 
 HEADS = 6
 MID_RATE = 4
@@ -108,7 +109,7 @@
     scale = head_dim ** (-0.5)
     qkv = jnp.dot(
         normed,
-        lax.all_gather(qkv_weight, "dp", axis=0, tiled=True),
+        jnp.concatenate(all_to_all(jnp.stack([qkv_weight] * axis_size("dp")), "dp", 0, 0), axis=0),
         preferred_element_type=jnp.float32,
     ).astype(jnp.bfloat16)
     queries = qkv[:, :width].reshape(tok_dev, heads_n, head_dim)

time: 175 us -> 229 us (1.31)
  waiting for transfers between devices: 123 us -> 167 us
  starting transfers between devices: 1.66 us -> 9.06 us
  local copies, waits for them, and re-layouts: 9.92 us -> 14.4 us
  other arithmetic: 14.2 us -> 11.9 us
    all_to_all x0 -> x1, waiting for transfers between devices: none -> 149 us  [local(): all_to_all(jnp.stack([qkv_weight] * axis_size('dp')), 'dp', 0, 0)]
    all_gather x1 -> x0, waiting for transfers between devices: 105 us -> none  [local(): lax.all_gather(qkv_weight, 'dp', axis=0, tiled=True)]
    all_to_all x0 -> x1, starting transfers between devices: none -> 7.42 us  [local(): all_to_all(jnp.stack([qkv_weight] * axis_size('dp')), 'dp', 0, 0)]
    another operation x0 -> x1, local copies, waits for them, and re-layouts: none -> 4.56 us  [local(): jnp.stack([qkv_weight] * axis_size('dp'))]
  transfers between devices with their start and end apart: 4 -> 4, of which waited for: 2 -> 2; matrix products, arithmetic and copies ran while one was open for 11% -> 7% of each run, Pallas kernels for 0% -> 0%
where the time goes in v1:
time: 229 us; the launch traced here: 228 us
  waiting for transfers between devices  167 us (73%)
  local copies, waits for them, and re-layouts  14.4 us (6%)
  between operations  13.9 us (6%)
  matrix products  12 us (5%)
  other arithmetic  11.9 us (5%)
  starting transfers between devices  9.06 us (4%)
    all_to_all x1, waiting for transfers between devices, local(): all_to_all(jnp.stack([qkv_weight] * axis_size('dp')), 'dp', 0, 0)  149 us
    ppermute x2, waiting for transfers between devices, from_partner(): return lax.ppermute(value, axis, pairs)  18.2 us
    all_to_all x1, starting transfers between devices, local(): all_to_all(jnp.stack([qkv_weight] * axis_size('dp')), 'dp', 0, 0)  7.42 us
    dot_general x1, matrix products, local(): jnp.dot(normed, jnp.concatenate(all_to_all(jnp.stack([qkv_weight] * axis_...  6.07 us
  transfers between devices with their start and end apart: 4, of which 2 were waited for; matrix products, arithmetic and copies ran while one was open for 7% of the time, Pallas kernels for 0%

profile of v1, /device:TPU:0, one launch (start us, length us, event | category | flops | bytes accessed | tf_op | source)
XLA Modules:
  0.0 228.3 jit_solution(5045058478346879001)
XLA Ops:
  6.5 4.6 %stack.18 = bf16[8,192,2304]{2,1,0:T(8,128)(2,1)} broadcast(bf16[192,2304]{1,0:T(8,128)(2,1)} %param.9), dimensions={1,2} | broadcast | bytes 7962624 | tf_op jit(solution)/shard_map/stack | solution.py:112
  11.1 0.0 copy-start
  11.1 7.4 %all-to-all-start = ((bf16[8,192,2304]{2,1,0:T(8,128)(2,1)}), bf16[8,192,2304]{2,1,0:T(8,128)(2,1)}, u32[]{:S(2)}, u32[]{:S(2)}) async-start(bf16[8,192,2304]{2,1,0:T(8,128)(2,1)} %stack.18), calls=%async_computation | async-start | bytes 14155776 | tf_op jit(solution)/shard_map/all_to_all | solution.py:112
  18.5 0.0 all-gather.2.cloned.1.call-start
  18.6 0.1 mul.123
  18.7 0.6 iota_compare_fusion.2
  19.4 0.2 mul.131
  19.6 0.1 add_xor_fusion
  19.6 0.7 fusion.38
  20.3 1.1 iota_compare_fusion.3
  21.5 0.6 fusion.48
  22.1 1.3 add_select_fusion
  23.4 0.1 select_reduce_fusion.1
  23.5 0.2 convert_reduce_fusion
  23.7 0.5 fusion.8
  24.2 0.7 add_compare_fusion.1
  24.8 148.8 %all-to-all-done = bf16[8,192,2304]{2,1,0:T(8,128)(2,1)} async-done(((bf16[8,192,2304]{2,1,0:T(8,128)(2,1)}), bf16[8,192,2304]{2,1,0:T(8,128)(2,1)}, u32[]{:S(2)}, u32[]{:S(2)}) %all-to-all-start) | async-done | bytes 7077920 | tf_op jit(solution)/shard_map/all_to_all | solution.py:112
  173.6 6.1 %convolution_convert_fusion = bf16[384,2304]{1,0:T(8,128)(2,1)S(1)} fusion(bf16[1536,2304]{1,0:T(8,128)(2,1)} %bitcast.3, bf16[1,384,1536]{2,1,0:T(8,128)(2,1)S(1)} %copy-done, f32[1536]{0:T(1024)S(1)} %copy-done.12, f32[384]{0:T(512)S(1)} %add_rsqrt_fusion, f32[384]{0:T(512)S(1)} %broadcast_multiply_fusion.2), kind=kOutput, calls=%fused_computation | convolution fusion | flops 2721742848 | bytes 10036224 | tf_op jit(solution)/shard_map/dot_general | solution.py:110
  179.7 0.1 fusion.44
  179.8 0.7 reshape_reshape.14
  180.5 0.3 fusion.47
  180.8 0.7 reshape_reshape.13
  181.5 0.3 fusion.46
  181.9 0.7 pad_maximum_fusion.2
  182.7 0.0 collective-permute-start
  182.7 0.0 all-gather.2.cloned.1.call-update
  182.7 0.3 copy.82
  183.0 0.7 reshape_reshape.12
  183.7 0.3 copy.80
  184.0 0.3 copy.102
  184.3 0.9 fusion.45
  185.2 0.3 copy.83
  185.5 0.3 copy.81
  185.9 1.1 copy.103
  186.9 0.0 copy-done.4
  187.0 0.7 fusion.1
  187.7 0.0 copy-start.1
  187.7 0.8 fusion.2
  188.6 0.0 collective-permute-done
  188.6 1.0 pad_maximum_fusion.1
  189.6 1.6 collective-permute-start.1
  191.2 1.3 fusion.10
  192.5 18.2 %collective-permute-done.1 = bf16[2,6,192,128]{3,2,1,0:T(8,128)(2,1)S(1)} collective-permute-done((bf16[2,6,192,128]{3,2,1,0:T(8,128)(2,1)S(1)}, bf16[2,6,192,128]{3,2,1,0:T(8,128)(2,1)S(1)}, u32[]{:S(2)}, u32[]{:S(2)}) %collective-permute-start.1) | collective-permute-done | bytes 589856 | tf_op jit(solution)/shard_map/ppermute | solution.py:16
  210.7 1.0 pad_maximum_fusion
  211.7 0.5 fusion.49
  212.2 0.4 fusion.20
  212.6 0.6 fusion.23
  213.2 0.0 all-gather.2.cloned.1.call-done
  213.2 1.5 fusion.50
  214.7 0.4 fusion.21
  215.1 0.0 copy-done.7
  215.1 0.2 broadcast_select_fusion.1
  215.3 0.2 select_n.153
  215.5 0.2 select_n.151
  215.7 0.2 select_n.152
  215.9 0.2 select_n.145
  216.1 1.4 fusion.22
  217.6 0.2 mul.128
  217.8 0.2 mul.134
  218.0 0.4 broadcast_multiply_fusion.1
  218.4 1.2 fusion
  219.7 0.4 fusion.16
  220.1 0.3 copy.105
  220.4 1.1 copy.106
  (50 shorter events, 0.3 us)
Async XLA Ops:
  11.1 8.5 %copy-start.8 = (s32[1,4]{1,0:T(1,128)S(1)}, s32[1,4]{1,0:T(1,128)}, u32[]{:S(2)}) copy-start(s32[1,4]{1,0:T(1,128)} %param.7) | copy-start | bytes 52
  11.1 11.0 %copy-start.9 = (pred[384]{0:T(512)(128)(4,1)S(1)}, pred[384]{0:T(512)(128)(4,1)}, u32[]{:S(2)}) copy-start(pred[384]{0:T(512)(128)(4,1)} %constant.173) | copy-start | bytes 1156
  11.1 11.0 %copy-start.10 = (pred[384]{0:T(512)(128)(4,1)S(1)}, pred[384]{0:T(512)(128)(4,1)}, u32[]{:S(2)}) copy-start(pred[384]{0:T(512)(128)(4,1)} %constant.174) | copy-start | bytes 1156
  11.1 11.0 %copy-start.11 = (pred[384]{0:T(512)(128)(4,1)S(1)}, pred[384]{0:T(512)(128)(4,1)}, u32[]{:S(2)}) copy-start(pred[384]{0:T(512)(128)(4,1)} %constant.175) | copy-start | bytes 1156
  11.1 12.3 %copy-start = (bf16[1,384,1536]{2,1,0:T(8,128)(2,1)S(1)}, bf16[1,384,1536]{2,1,0:T(8,128)(2,1)}, u32[]{:S(2)}) copy-start(bf16[1,384,1536]{2,1,0:T(8,128)(2,1)} %param.6) | copy-start | bytes 3538948
  11.1 162.5 %all-to-all-start = ((bf16[8,192,2304]{2,1,0:T(8,128)(2,1)}), bf16[8,192,2304]{2,1,0:T(8,128)(2,1)}, u32[]{:S(2)}, u32[]{:S(2)}) async-start(bf16[8,192,2304]{2,1,0:T(8,128)(2,1)} %stack.18), calls=%async_computation | async-start | bytes 14155776 | tf_op jit(solution)/shard_map/all_to_all | solution.py:112
  18.5 155.1 %copy-start.12 = (f32[1536]{0:T(1024)S(1)}, f32[1536]{0:T(1024)}, u32[]{:S(2)}) copy-start(f32[1536]{0:T(1024)} %param.8) | copy-start | bytes 18436
  18.5 194.6 %all-gather.2.cloned.1.call-start = ((), (), s32[]{:S(2)}) async-start(), calls=%async_computation.1 | async-start | bytes 1474560 | tf_op jit(solution)/shard_map/all_gather | solution.py:147
  182.7 5.9 %collective-permute-start = (bf16[2,6,96,128]{3,2,1,0:T(8,128)(2,1)}, bf16[2,6,96,128]{3,2,1,0:T(8,128)(2,1)}, u32[]{:S(2)}, u32[]{:S(2)}) collective-permute-start(bf16[2,6,96,128]{3,2,1,0:T(8,128)(2,1)} %pad_maximum_fusion.2), channel_id=1, source_target_pairs={{0,1},{1,0},{2,3},{3,2},{4,5},{5,4},{6,7},{7,6},{8,9},{9,8},{10,11... | collective-permute-start | bytes 884744 | tf_op jit(solution)/shard_map/ppermute | solution.py:16
  185.2 1.7 copy-start.4
  185.2 1.7 copy-start.3
  185.2 1.8 copy-start.2
  185.2 1.8 copy-start.6
  187.7 3.5 %copy-start.1 = (bf16[384,6,128]{2,0,1:T(8,128)(2,1)S(1)}, bf16[384,6,128]{2,0,1:T(8,128)(2,1)}, u32[]{:S(2)}) copy-start(bf16[384,6,128]{2,0,1:T(8,128)(2,1)} %copy.103) | copy-start | bytes 1769476
  189.6 21.1 %collective-permute-start.1 = (bf16[2,6,192,128]{3,2,1,0:T(8,128)(2,1)S(1)}, bf16[2,6,192,128]{3,2,1,0:T(8,128)(2,1)S(1)}, u32[]{:S(2)}, u32[]{:S(2)}) collective-permute-start(bf16[2,6,192,128]{3,2,1,0:T(8,128)(2,1)S(1)} %pad_maximum_fusion.1), channel_id=1, source_target_pairs={{0,2},{1,3},{2,0},{3,1},{4,6},{5,7},{6,4},{7,5},{8,10},{9,11},{10,... | collective-permute-start | bytes 1769480 | tf_op jit(solution)/shard_map/ppermute | solution.py:16
  192.5 19.2 %copy-start.5 = (pred[6,384]{1,0:T(8,128)(4,1)S(1)}, pred[6,384]{1,0:T(8,128)(4,1)}, u32[]{:S(2)}) copy-start(pred[6,384]{1,0:T(8,128)(4,1)} %get-tuple-element.50) | copy-start | bytes 6916
  213.1 2.0 copy-start.7
Sparse Core Ops, SparseCore 0:
  182.8 22.1 all-gather.1
